TPU v7x, 32 devices: a whole 2x2x4 slice. The times are simulated.
32 devices in a mesh: dom: 16 (over z, y, core), feat: 2 (over x).
Axes of the slice: x: 2, y: 2, z: 4, core: 2. Of those that a mesh axis runs over, the one named last changes fastest.
Arguments:
- features: bfloat16 [256, 8192], P('feat', 'dom'), may hold values from -6 to 6
- in_degree: int32 [8192], P('dom'), may hold values from 16 to 64
- send_rows: int32 [16, 16, 16], P('dom'), may hold values from 0 to 511
- send_count: int32 [16, 16], P('dom'), may hold values from 0 to 16, as said below
- hub_owner: int32 [4], replicated, may hold values from 0 to 15, as said below
- hub_rows: int32 [4, 128], replicated, may hold values from 0 to 511
- local_dest: int32 [256], P('dom'), may hold values from 0 to 3
- local_source: int32 [256], P('dom'), may hold values from 0 to 3
- local_tiles: bfloat16 [256, 128, 128], P('dom'), may hold values from 0 to 1
- border_dest: int32 [256], P('dom'), may hold values from 0 to 3
- border_source: int32 [256], P('dom'), may hold values from 0 to 1
- border_tiles: bfloat16 [256, 128, 128], P('dom'), may hold values from 0 to 1
- hub_dest: int32 [256], P('dom'), may hold values from 0 to 3
- hub_source: int32 [256], P('dom'), may hold values from 0 to 3
- hub_tiles: bfloat16 [256, 128, 128], P('dom'), may hold values from 0 to 1
- self_weight: bfloat16 [256, 256], P('feat'), may hold values from -0.375 to 0.375
- neighbor_weight: bfloat16 [256, 256], P('feat'), may hold values from -0.375 to 0.375
- out_bias: float32 [256], P('feat'), may hold values from -3 to 3
Outputs:
- updated: bfloat16 [256, 8192], P('feat', 'dom')
Inputs may be any that keep to these rules, and one draw needn't show every extreme that they name: send_count[q, p] of the 16 slots from q to p are live; in every draw some destinations receive 16 live rows from every source. Hub block b belongs to partition hub_owner[b]; one partition owns exactly 2 blocks, every other partition at most one.
All inputs are finite; a program needn't handle non-finite values.
Results may differ from a plain program's by a relative error of at most 0.0034.
Values may be sent and summed in bfloat16 or wider, within the bound.
No kernel may reach another device: no remote copies, remote signals or barrier semaphores. Data moves between devices by JAX's collectives and lax.ppermute only.
A program may use at most 64 MiB of HBM per device.

v0:
```python
import jax
import jax.numpy as jnp
from jax import lax
from jax.sharding import PartitionSpec as P

HOWN = 2


def tile_terms(blocks, targets, source, tile_values, row_blocks):
    picked = jnp.take(blocks, source, axis=1)
    partial_value = jnp.einsum(
        "ftk,tik->fti", picked, tile_values, preferred_element_type=jnp.float32
    )
    onehot = (targets[:, None] == jnp.arange(row_blocks, dtype=jnp.int32)[None, :]).astype(
        jnp.float32
    )
    return jnp.einsum("fti,tr->fri", partial_value, onehot, precision=lax.Precision.HIGHEST)


def shards(
    features,
    in_degree,
    send_rows,
    send_count,
    hub_owner,
    hub_rows,
    local_dest,
    local_source,
    local_tiles,
    border_dest,
    border_source,
    border_tiles,
    hub_dest,
    hub_source,
    hub_tiles,
    self_weight,
    neighbor_weight,
    out_bias,
):
    feat_rows, vertex_count = features.shape
    tile_size = local_tiles.shape[1]
    row_blocks = vertex_count // tile_size
    partitions = lax.axis_size("dom")
    capacity = send_rows.shape[2]
    own_blocks = features.reshape(feat_rows, row_blocks, tile_size)
    local_sum = tile_terms(own_blocks, local_dest, local_source, local_tiles, row_blocks)
    pick_rows = send_rows[0].reshape(-1)
    outgoing = jnp.take(features, pick_rows, axis=1).reshape(feat_rows, partitions, capacity)
    alive_slots = (jnp.arange(capacity, dtype=jnp.int32)[None, :] < send_count[0][:, None]).astype(
        jnp.bfloat16
    )
    outgoing = outgoing * alive_slots[None]
    incoming = lax.all_to_all(outgoing, "dom", split_axis=1, concat_axis=1, tiled=True)
    border_blocks = incoming.reshape(feat_rows, partitions * capacity // tile_size, tile_size)
    border_sum = tile_terms(border_blocks, border_dest, border_source, border_tiles, row_blocks)
    hub_count = hub_owner.shape[0]
    position = lax.axis_index("dom")
    block_ids = jnp.arange(hub_count, dtype=jnp.int32)
    earlier = block_ids[:, None] > block_ids[None, :]
    same_owner = hub_owner[:, None] == hub_owner[None, :]
    order_rank = jnp.sum((earlier & same_owner).astype(jnp.int32), axis=1)
    owned_here = hub_owner == position
    choose = (
        owned_here[None, :] & (order_rank[None, :] == jnp.arange(HOWN, dtype=jnp.int32)[:, None])
    ).astype(jnp.int32)
    slot_rows = jnp.sum(choose[:, :, None] * hub_rows[None], axis=1)
    owned_blocks = jnp.take(features, slot_rows.reshape(-1), axis=1).reshape(
        feat_rows, HOWN, tile_size
    )
    everyone = lax.all_gather(owned_blocks, "dom", axis=1, tiled=True)
    hub_blocks = jnp.take(everyone, hub_owner * HOWN + order_rank, axis=1)
    hub_sum = tile_terms(hub_blocks, hub_dest, hub_source, hub_tiles, row_blocks)
    degree = in_degree.astype(jnp.float32).reshape(row_blocks, tile_size)
    aggregate = (
        ((local_sum + border_sum + hub_sum) / degree[None])
        .astype(jnp.bfloat16)
        .reshape(feat_rows, vertex_count)
    )
    running = jnp.dot(
        self_weight,
        lax.all_gather(features, "feat", axis=0, tiled=True),
        preferred_element_type=jnp.float32,
    )
    combined = running + jnp.dot(
        neighbor_weight,
        lax.all_gather(aggregate, "feat", axis=0, tiled=True),
        preferred_element_type=jnp.float32,
    )
    return jnp.maximum(combined + out_bias[:, None], 0.0).astype(jnp.bfloat16)


def solution(mesh):
    placed = (
        P("feat", "dom"),
        P("dom"),
        P("dom", None, None),
        P("dom", None),
        P(),
        P(),
        P("dom"),
        P("dom"),
        P("dom", None, None),
        P("dom"),
        P("dom"),
        P("dom", None, None),
        P("dom"),
        P("dom"),
        P("dom", None, None),
        P("feat", None),
        P("feat", None),
        P("feat"),
    )
    return jax.shard_map(
        shards, mesh=mesh, in_specs=placed, out_specs=P("feat", "dom"), check_vma=False
    )
```

profile of v0, /device:TPU:0, one launch (start us, length us, event | category | flops | bytes accessed | tf_op | source)
XLA Modules:
  0.0 80.8 jit_solution(9627374421501627303)
XLA Ops:
  6.5 0.8 %reshape_squeeze.3 = s32[256]{0:T(256)S(1)} reshape(s32[1,16,16]{2,1,0:T(8,128)} %param.24) | data formatting | bytes 2048 | tf_op jit(solution)/shard_map/reshape;squeeze | solution.py:47
  7.4 1.0 %copy.61 = bf16[128,512]{0,1:T(8,128)(2,1)S(1)} copy(bf16[128,512]{1,0:T(8,128)(2,1)} %param.22) | data formatting | bytes 262144 | tf_op args[0]
  8.4 0.6 copy-done.11
  9.2 0.9 %gather_fusion.3 = bf16[256,128]{1,0:T(8,128)(2,1)S(1)} fusion(bf16[128,512]{0,1:T(8,128)(2,1)S(1)} %copy.61, s32[1024]{0:T(1024)S(1)} %pad_clamp_fusion.4), kind=kCustom, calls=%fused_computation.1.clone | custom fusion | bytes 132096 | tf_op jit(solution)/shard_map/jit(_take)/gather | solution.py:48
  10.1 0.7 broadcast_multiply_fusion
  10.9 7.4 %all-to-all-start = ((bf16[128,16,16]{0,2,1:T(8,128)(2,1)}), bf16[128,16,16]{0,2,1:T(8,128)(2,1)S(1)}, u32[]{:S(2)}, u32[]{:S(2)}) async-start(bf16[128,16,16]{0,2,1:T(8,128)(2,1)} %broadcast_multiply_fusion), calls=%async_computation | async-start | bytes 131072 | tf_op jit(solution)/shard_map/all_to_all | solution.py:53
  18.3 0.6 copy-done.12
  18.9 0.2 convert_reduce_fusion
  19.1 0.7 copy-done.6
  19.9 0.9 %gather_fusion.4 = bf16[256,128]{1,0:T(8,128)(2,1)S(1)} fusion(bf16[128,512]{0,1:T(8,128)(2,1)S(1)} %copy.61, s32[1024]{0:T(1024)S(1)} %pad_clamp_fusion.2), kind=kCustom, calls=%fused_computation.3.clone | custom fusion | bytes 132096 | tf_op jit(solution)/shard_map/jit(_take)/gather | solution.py:67
  20.9 0.7 copy.68
  21.6 0.6 copy-done.13
  22.3 0.6 copy-done.14
  23.1 0.6 gather_fusion.2
  23.8 0.6 copy-done.7
  24.5 0.5 convolution_bitcast_fusion.2
  25.1 1.1 %fusion.7 = f32[4,128,128]{2,0,1:T(4,128)S(1)} fusion(f32[128,16,128]{2,0,1:T(8,128)S(1)} %convolution_bitcast_fusion.2, s32[16]{0:T(128)S(1)} %copy-done.8), kind=kOutput, calls=%fused_computation.20 | convolution fusion | flops 12582976 | bytes 1310784 | tf_op jit(solution)/shard_map/fti,tr->fri/dot_general | solution.py:17
  26.2 6.5 %all_gather.9 = bf16[256,512]{1,0:T(8,128)(2,1)S(1)} all-gather(bf16[128,512]{1,0:T(8,128)(2,1)S(1)} %copy-done.3), channel_id=1, replica_groups=mesh['dom'=16,'feat'=2] {'feat'}, dimensions={0}, use_global_device_ids=true | all-gather | bytes 393216 | tf_op jit(solution)/shard_map/all_gather | solution.py:81
  32.9 0.6 gather_fusion
  33.5 0.4 copy-done.1
  33.9 0.5 convolution_bitcast_fusion.1
  34.6 1.1 %convolution_add_fusion.1 = f32[4,128,128]{2,0,1:T(4,128)S(1)} fusion(f32[4,128,128]{2,0,1:T(4,128)S(1)} %fusion.7, f32[128,16,128]{2,0,1:T(8,128)S(1)} %convolution_bitcast_fusion.1, s32[16]{0:T(128)S(1)} %copy-done.9), kind=kOutput, calls=%fused_computation.10 | convolution fusion | flops 12648512 | bytes 1572928 | tf_op jit(solution)/shard_map/fti,tr->fri/dot_general | solution.py:17
  35.6 25.4 %all-gather.2.cloned.1.call-done = bf16[128,32,128]{2,0,1:T(8,128)(2,1)} async-done(((bf16[128,2,128]{2,0,1:T(8,128)(2,1)}), bf16[128,32,128]{2,0,1:T(8,128)(2,1)}) %all-gather.2.cloned.1.call-update) | async-done | bytes 1048592 | tf_op jit(solution)/shard_map/all_gather | solution.py:70
  61.0 1.8 %gather_fusion.1 = bf16[4,128,128]{2,1,0:T(8,128)(2,1)S(1)} fusion(bf16[128,32,128]{2,0,1:T(8,128)(2,1)} %all-gather.2.cloned.1.call-done, s32[1024]{0:T(1024)S(1)} %pad_clamp_fusion.1), kind=kCustom, calls=%fused_computation.5 | custom fusion | bytes 262160 | tf_op jit(solution)/shard_map/jit(_take)/gather | solution.py:71
  62.9 0.6 gather_fusion.5
  63.6 0.4 copy-done.2
  64.0 0.5 convolution_bitcast_fusion
  64.6 1.1 %fusion.3 = bf16[4,128,128]{2,0,1:T(4,128)(2,1)S(1)} fusion(f32[4,128,128]{2,0,1:T(4,128)S(1)} %convolution_add_fusion.1, f32[128,16,128]{2,0,1:T(8,128)S(1)} %convolution_bitcast_fusion, f32[4,128]{1,0:T(4,128)S(1)} %convert_bitcast_fusion, s32[16]{0:T(128)S(1)} %copy-done.16), kind=kOutput, calls=%fused_computation.16 | convolution fusion | flops 12779584 | bytes 1443904 | tf_op jit(solution)/shard_map/fti,tr->fri/dot_general | solution.py:17
  65.7 6.5 %all_gather.11 = bf16[256,512]{1,0:T(8,128)(2,1)S(1)} all-gather(bf16[128,512]{1,0:T(8,128)(2,1)S(1)} %bitcast.56), channel_id=1, replica_groups=mesh['dom'=16,'feat'=2] {'feat'}, dimensions={0}, use_global_device_ids=true | all-gather | bytes 393216 | tf_op jit(solution)/shard_map/all_gather | solution.py:86
  72.2 0.2 convolution_bitcast_fusion.3
  72.4 0.6 copy-done.5
  73.1 0.8 %fusion.4 = bf16[128,512]{1,0:T(8,128)(2,1)} fusion(f32[128,512]{1,0:T(8,128)S(1)} %convolution_bitcast_fusion.3, bf16[128,256]{1,0:T(8,128)(2,1)S(1)} %copy-done.5, bf16[256,512]{1,0:T(8,128)(2,1)S(1)} %all_gather.9, f32[128]{0:T(128)S(1)} %copy-done.10), kind=kOutput, calls=%fused_computation.17 | convolution fusion | flops 33816576 | bytes 721408 | tf_op jit(solution)/shard_map/dot_general | solution.py:79
  (55 shorter events, 1.3 us)
Async XLA Ops:
  6.5 17.9 %copy-start = (bf16[16,128,128]{2,1,0:T(8,128)(2,1)S(1)}, bf16[16,128,128]{2,1,0:T(8,128)(2,1)}, u32[]{:S(2)}) copy-start(bf16[16,128,128]{2,1,0:T(8,128)(2,1)} %param.30) | copy-start | bytes 1572868
  8.4 0.7 copy-start.11
  10.9 21.9 %all-to-all-start = ((bf16[128,16,16]{0,2,1:T(8,128)(2,1)}), bf16[128,16,16]{0,2,1:T(8,128)(2,1)S(1)}, u32[]{:S(2)}, u32[]{:S(2)}) async-start(bf16[128,16,16]{0,2,1:T(8,128)(2,1)} %broadcast_multiply_fusion), calls=%async_computation | async-start | bytes 131072 | tf_op jit(solution)/shard_map/all_to_all | solution.py:53
  18.3 0.7 copy-start.12
  18.3 42.8 %all-gather.2.cloned.1.call-start = ((), (), s32[]{:S(2)}) async-start(), calls=%async_computation.1 | async-start | bytes 1114112 | tf_op jit(solution)/shard_map/all_gather | solution.py:70
  19.1 0.7 copy-start.6
  21.6 0.7 copy-start.13
  22.3 0.7 copy-start.14
  23.1 0.7 copy-start.15
  23.8 0.7 copy-start.7
  24.5 0.7 copy-start.8
  25.1 1.1 %copy-start.3 = (bf16[128,512]{1,0:T(8,128)(2,1)S(1)}, bf16[128,512]{1,0:T(8,128)(2,1)}, u32[]{:S(2)}) copy-start(bf16[128,512]{1,0:T(8,128)(2,1)} %param.22) | copy-start | bytes 393220
  32.9 1.0 %copy-start.1 = (bf16[16,128,128]{2,1,0:T(8,128)(2,1)S(1)}, bf16[16,128,128]{2,1,0:T(8,128)(2,1)}, u32[]{:S(2)}) copy-start(bf16[16,128,128]{2,1,0:T(8,128)(2,1)} %param.33) | copy-start | bytes 1572868
  33.9 0.7 copy-start.9
  62.9 1.0 %copy-start.2 = (bf16[16,128,128]{2,1,0:T(8,128)(2,1)S(1)}, bf16[16,128,128]{2,1,0:T(8,128)(2,1)}, u32[]{:S(2)}) copy-start(bf16[16,128,128]{2,1,0:T(8,128)(2,1)} %param.36) | copy-start | bytes 1572868
  64.0 0.7 copy-start.16
  65.7 6.5 %copy-start.4 = (bf16[128,256]{1,0:T(8,128)(2,1)S(1)}, bf16[128,256]{1,0:T(8,128)(2,1)}, u32[]{:S(2)}) copy-start(bf16[128,256]{1,0:T(8,128)(2,1)} %param.38) | copy-start | bytes 196612
  72.2 0.8 %copy-start.5 = (bf16[128,256]{1,0:T(8,128)(2,1)S(1)}, bf16[128,256]{1,0:T(8,128)(2,1)}, u32[]{:S(2)}) copy-start(bf16[128,256]{1,0:T(8,128)(2,1)} %param.37) | copy-start | bytes 196612
  72.2 0.8 %copy-start.10 = (f32[128]{0:T(128)S(1)}, f32[128]{0:T(128)}, u32[]{:S(2)}) copy-start(f32[128]{0:T(128)} %param.39) | copy-start | bytes 1540
Sparse Core Ops, SparseCore 0:
  21.7 39.2 all-gather.1
where the time goes:
time: 81.3 us; the launch traced here: 80.8 us
  waiting for transfers between devices  25.4 us (31%)
  local copies, waits for them, and re-layouts  14 us (17%)
  between operations  13.7 us (17%)
  blocking collectives  13 us (16%)
  starting transfers between devices  7.43 us (9%)
  matrix products  5.75 us (7%)
  other arithmetic  1.48 us (2%)
    all_gather x1, waiting for transfers between devices, shards(): everyone = lax.all_gather(owned_blocks, 'dom', axis=1, tiled=True)  25.4 us
    all_to_all x1, starting transfers between devices, shards(): lax.all_to_all(outgoing, 'dom', split_axis=1, concat_axis=1, tiled=True)  7.38 us
    unnamed x36, local copies, waits for them, and re-layouts  6.71 us
    all_gather x1, blocking collectives, shards(): lax.all_gather(features, 'feat', axis=0, tiled=True)  6.51 us
    all_gather x1, blocking collectives, shards(): lax.all_gather(aggregate, 'feat', axis=0, tiled=True)  6.47 us
    dot_general x3, matrix products, tile_terms(): jnp.einsum('fti,tr->fri', partial_value, onehot, precision=lax.Precision....  3.16 us
    gather x3, local copies, waits for them, and re-layouts, tile_terms(): picked = jnp.take(blocks, source, axis=1)  1.94 us
    gather x1, local copies, waits for them, and re-layouts, shards(): hub_blocks = jnp.take(everyone, hub_owner * HOWN + order_rank, axis=1)  1.79 us
  transfers between devices with their start and end apart: 2, of which 1 were waited for; matrix products, arithmetic and copies ran while one was open for 8% of the time, Pallas kernels for 0%

commit v1 on v0

--- a/solution.py
+++ b/solution.py
@@ -2,8 +2,21 @@
 import jax.numpy as jnp
 from jax import lax
 from jax.sharding import PartitionSpec as P
+from jax.lax import axis_index, axis_size, ppermute
 
 HOWN = 2
+
+
+def files_list(vec, dim_i, xs):
+    everything = vec.shape
+    val = vec.reshape(*everything[:dim_i], xs, everything[dim_i] // xs, *everything[dim_i + 1 :])
+    return jnp.moveaxis(val, dim_i, 0)
+
+
+def produce_quarters_all(piece_in, axis_no):
+    value_now = list(piece_in.shape[1:])
+    value_now[axis_no] *= piece_in.shape[0]
+    return jnp.moveaxis(piece_in, 0, axis_no).reshape(value_now)
 
 
 def tile_terms(blocks, targets, source, tile_values, row_blocks):
@@ -50,7 +63,14 @@
         jnp.bfloat16
     )
     outgoing = outgoing * alive_slots[None]
-    incoming = lax.all_to_all(outgoing, "dom", split_axis=1, concat_axis=1, tiled=True)
+    long_array, y1 = (axis_size("dom"), axis_index("dom"))
+    outcome_arr = files_list(outgoing, 1, long_array)
+    by_place = [outcome_arr[y1]]
+    for b in tuple(range(1, long_array)):
+        f_next = outcome_arr[y1 ^ b]
+        by_place.append(ppermute(f_next, "dom", [(tick, tick ^ b) for tick in range(long_array)]))
+    outcome_arr = jnp.stack(by_place, 0)[y1 ^ jnp.arange(long_array)]
+    incoming = produce_quarters_all(outcome_arr, 1)
     border_blocks = incoming.reshape(feat_rows, partitions * capacity // tile_size, tile_size)
     border_sum = tile_terms(border_blocks, border_dest, border_source, border_tiles, row_blocks)
     hub_count = hub_owner.shape[0]

time: 81.3 us -> 77.9 us (0.958)
  waiting for transfers between devices: 25.4 us -> 7.17 us
  starting transfers between devices: 7.43 us -> 22.1 us
    all_gather x1, waiting for transfers between devices: 25.4 us -> 1.48 us  [shards(): everyone = lax.all_gather(owned_blocks, 'dom', axis=1, tiled=True)]
    ppermute x0 -> x15, starting transfers between devices: none -> 22.1 us  [shards(): ppermute(f_next, 'dom', [(tick, tick ^ b) for tick in range(long_array)])]
    all_to_all x1 -> x0, starting transfers between devices: 7.38 us -> none  [shards(): lax.all_to_all(outgoing, 'dom', split_axis=1, concat_axis=1, tiled=True)]
    ppermute x0 -> x15, waiting for transfers between devices: none -> 5.68 us  [shards(): ppermute(f_next, 'dom', [(tick, tick ^ b) for tick in range(long_array)])]
    unnamed x36 -> x53, local copies, waits for them, and re-layouts: 6.71 us -> 7.53 us
  transfers between devices with their start and end apart: 2 -> 16, of which waited for: 1 -> 3; matrix products, arithmetic and copies ran while one was open for 8% -> 9% of each run, Pallas kernels for 0% -> 0%
where the time goes in v1:
time: 77.9 us; the launch traced here: 77.4 us
  starting transfers between devices  22.1 us (28%)
  local copies, waits for them, and re-layouts  14.7 us (19%)
  between operations  13.9 us (18%)
  blocking collectives  12.9 us (17%)
  waiting for transfers between devices  7.17 us (9%)
  matrix products  5.77 us (7%)
  other arithmetic  0.82 us (1%)
    ppermute x15, starting transfers between devices, shards(): ppermute(f_next, 'dom', [(tick, tick ^ b) for tick in range(long_array)])  22.1 us
    unnamed x53, local copies, waits for them, and re-layouts  7.53 us
    all_gather x1, blocking collectives, shards(): lax.all_gather(aggregate, 'feat', axis=0, tiled=True)  6.47 us
    all_gather x1, blocking collectives, shards(): lax.all_gather(features, 'feat', axis=0, tiled=True)  6.42 us
    ppermute x15, waiting for transfers between devices, shards(): ppermute(f_next, 'dom', [(tick, tick ^ b) for tick in range(long_array)])  5.68 us
    dot_general x3, matrix products, tile_terms(): jnp.einsum('fti,tr->fri', partial_value, onehot, precision=lax.Precision....  3.16 us
    gather x3, local copies, waits for them, and re-layouts, tile_terms(): picked = jnp.take(blocks, source, axis=1)  1.94 us
    gather x1, local copies, waits for them, and re-layouts, shards(): hub_blocks = jnp.take(everyone, hub_owner * HOWN + order_rank, axis=1)  1.79 us
  transfers between devices with their start and end apart: 16, of which 3 were waited for; matrix products, arithmetic and copies ran while one was open for 9% of the time, Pallas kernels for 0%

profile of v1, /device:TPU:0, one launch (start us, length us, event | category | flops | bytes accessed | tf_op | source)
XLA Modules:
  0.0 77.4 jit_solution(2698391043795979528)
XLA Ops:
  6.6 0.7 copy-done.14
  8.3 1.0 %copy.61 = bf16[128,512]{0,1:T(8,128)(2,1)S(1)} copy(bf16[128,512]{1,0:T(8,128)(2,1)} %param.22) | data formatting | bytes 262144 | tf_op args[0]
  9.4 0.6 copy-done.13
  10.1 0.9 %gather_fusion.4 = bf16[256,128]{1,0:T(8,128)(2,1)S(1)} fusion(bf16[128,512]{0,1:T(8,128)(2,1)S(1)} %copy.61, s32[1024]{0:T(1024)S(1)} %pad_clamp_fusion.5), kind=kCustom, calls=%fused_computation.1.clone | custom fusion | bytes 132096 | tf_op jit(solution)/shard_map/jit(_take)/gather | solution.py:61
  11.8 2.6 %collective-permute-start.1 = (bf16[128,1,16]{0,2,1:T(8,128)(2,1)S(1)}, bf16[128,1,16]{0,2,1:T(8,128)(2,1)S(1)}, u32[]{:S(2)}, u32[]{:S(2)}) collective-permute-start(bf16[128,1,16]{0,2,1:T(8,128)(2,1)S(1)} %get-tuple-element.22), channel_id=1, source_target_pairs={{0,4},{2,6},{4,0},{6,2},{8,12},{10,14},{12,8},{14,10},{16,20},{18,... | collective-permute-start | bytes 12296 | tf_op jit(solution)/shard_map/ppermute | solution.py:71
  14.5 1.8 %collective-permute-start.3 = (bf16[128,1,16]{0,2,1:T(8,128)(2,1)S(1)}, bf16[128,1,16]{0,2,1:T(8,128)(2,1)S(1)}, u32[]{:S(2)}, u32[]{:S(2)}) collective-permute-start(bf16[128,1,16]{0,2,1:T(8,128)(2,1)S(1)} %get-tuple-element.20), channel_id=1, source_target_pairs={{0,8},{2,10},{4,12},{6,14},{8,0},{10,2},{12,4},{14,6},{16,24},{18,... | collective-permute-start | bytes 12296 | tf_op jit(solution)/shard_map/ppermute | solution.py:71
  16.3 0.9 %gather_fusion.5 = bf16[256,128]{1,0:T(8,128)(2,1)S(1)} fusion(bf16[128,512]{0,1:T(8,128)(2,1)S(1)} %copy.61, s32[1024]{0:T(1024)S(1)} %pad_clamp_fusion.2), kind=kCustom, calls=%fused_computation.3.clone | custom fusion | bytes 132096 | tf_op jit(solution)/shard_map/jit(_take)/gather | solution.py:87
  17.3 0.7 copy.68
  18.1 0.6 copy-done.15
  18.7 0.6 copy-done.9
  19.4 0.6 copy-done.16
  20.2 0.7 copy-done.8
  20.9 0.6 gather_fusion.3
  22.2 1.1 %fusion.7 = f32[4,128,128]{2,0,1:T(4,128)S(1)} fusion(f32[128,16,128]{2,0,1:T(8,128)S(1)} %convolution_bitcast_fusion.2, s32[16]{0:T(128)S(1)} %copy-done.10), kind=kOutput, calls=%fused_computation.21 | convolution fusion | flops 12582976 | bytes 1310784 | tf_op jit(solution)/shard_map/fti,tr->fri/dot_general | solution.py:30
  23.3 6.4 %all_gather.9 = bf16[256,512]{1,0:T(8,128)(2,1)S(1)} all-gather(bf16[128,512]{1,0:T(8,128)(2,1)S(1)} %copy-done.3), channel_id=1, replica_groups=mesh['dom'=16,'feat'=2] {'feat'}, dimensions={0}, use_global_device_ids=true | all-gather | bytes 393216 | tf_op jit(solution)/shard_map/all_gather | solution.py:101
  29.7 2.7 %collective-permute-start.5 = (bf16[128,1,16]{0,2,1:T(8,128)(2,1)S(1)}, bf16[128,1,16]{0,2,1:T(8,128)(2,1)S(1)}, u32[]{:S(2)}, u32[]{:S(2)}) collective-permute-start(bf16[128,1,16]{0,2,1:T(8,128)(2,1)S(1)} %get-tuple-element.18), channel_id=1, source_target_pairs={{0,12},{2,14},{4,8},{6,10},{8,4},{10,6},{12,0},{14,2},{16,28},{18,... | collective-permute-start | bytes 12296 | tf_op jit(solution)/shard_map/ppermute | solution.py:71
  32.5 2.7 %collective-permute-start.7 = (bf16[128,1,16]{0,2,1:T(8,128)(2,1)S(1)}, bf16[128,1,16]{0,2,1:T(8,128)(2,1)S(1)}, u32[]{:S(2)}, u32[]{:S(2)}) collective-permute-start(bf16[128,1,16]{0,2,1:T(8,128)(2,1)S(1)} %get-tuple-element.16), channel_id=1, source_target_pairs={{0,16},{2,18},{4,20},{6,22},{8,24},{10,26},{12,28},{14,30},{16,0},... | collective-permute-start | bytes 12296 | tf_op jit(solution)/shard_map/ppermute | solution.py:71
  35.3 3.5 %collective-permute-start.9 = (bf16[128,1,16]{0,2,1:T(8,128)(2,1)S(1)}, bf16[128,1,16]{0,2,1:T(8,128)(2,1)S(1)}, u32[]{:S(2)}, u32[]{:S(2)}) collective-permute-start(bf16[128,1,16]{0,2,1:T(8,128)(2,1)S(1)} %get-tuple-element.14), channel_id=1, source_target_pairs={{0,20},{2,22},{4,16},{6,18},{8,28},{10,30},{12,24},{14,26},{16,4},... | collective-permute-start | bytes 12296 | tf_op jit(solution)/shard_map/ppermute | solution.py:71
  38.9 2.9 %collective-permute-start.11 = (bf16[128,1,16]{0,2,1:T(8,128)(2,1)S(1)}, bf16[128,1,16]{0,2,1:T(8,128)(2,1)S(1)}, u32[]{:S(2)}, u32[]{:S(2)}) collective-permute-start(bf16[128,1,16]{0,2,1:T(8,128)(2,1)S(1)} %get-tuple-element.12), channel_id=1, source_target_pairs={{0,24},{2,26},{4,28},{6,30},{8,16},{10,18},{12,20},{14,22},{16,8},... | collective-permute-start | bytes 12296 | tf_op jit(solution)/shard_map/ppermute | solution.py:71
  41.8 0.7 collective-permute-start.12
  42.5 4.4 %collective-permute-start.13 = (bf16[128,1,16]{0,2,1:T(8,128)(2,1)S(1)}, bf16[128,1,16]{0,2,1:T(8,128)(2,1)S(1)}, u32[]{:S(2)}, u32[]{:S(2)}) collective-permute-start(bf16[128,1,16]{0,2,1:T(8,128)(2,1)S(1)} %get-tuple-element.10), channel_id=1, source_target_pairs={{0,28},{2,30},{4,24},{6,26},{8,20},{10,22},{12,16},{14,18},{16,12}... | collective-permute-start | bytes 12296 | tf_op jit(solution)/shard_map/ppermute | solution.py:71
  47.1 1.8 %collective-permute-done.13 = bf16[128,1,16]{0,2,1:T(8,128)(2,1)S(1)} collective-permute-done((bf16[128,1,16]{0,2,1:T(8,128)(2,1)S(1)}, bf16[128,1,16]{0,2,1:T(8,128)(2,1)S(1)}, u32[]{:S(2)}, u32[]{:S(2)}) %collective-permute-start.13) | collective-permute-done | bytes 4128 | tf_op jit(solution)/shard_map/ppermute | solution.py:71
  48.9 3.9 %collective-permute-done.14 = bf16[128,1,16]{0,2,1:T(8,128)(2,1)S(1)} collective-permute-done((bf16[128,1,16]{0,2,1:T(8,128)(2,1)S(1)}, bf16[128,1,16]{0,2,1:T(8,128)(2,1)S(1)}, u32[]{:S(2)}, u32[]{:S(2)}) %collective-permute-start.14) | collective-permute-done | bytes 4128 | tf_op jit(solution)/shard_map/ppermute | solution.py:71
  53.5 0.6 gather_fusion.1
  55.2 1.1 %convolution_add_fusion.1 = f32[4,128,128]{2,0,1:T(4,128)S(1)} fusion(f32[4,128,128]{2,0,1:T(4,128)S(1)} %fusion.7, f32[128,16,128]{2,0,1:T(8,128)S(1)} %convolution_bitcast_fusion.1, s32[16]{0:T(128)S(1)} %copy-done.11), kind=kOutput, calls=%fused_computation.11 | convolution fusion | flops 12648512 | bytes 1572928 | tf_op jit(solution)/shard_map/fti,tr->fri/dot_general | solution.py:30
  56.2 1.5 %all-gather.2.cloned.1.call-done = bf16[128,32,128]{2,0,1:T(8,128)(2,1)} async-done(((bf16[128,2,128]{2,0,1:T(8,128)(2,1)}), bf16[128,32,128]{2,0,1:T(8,128)(2,1)}) %all-gather.2.cloned.1.call-update) | async-done | bytes 1048592 | tf_op jit(solution)/shard_map/all_gather | solution.py:90
  57.7 1.8 %gather_fusion.2 = bf16[4,128,128]{2,1,0:T(8,128)(2,1)S(1)} fusion(bf16[128,32,128]{2,0,1:T(8,128)(2,1)} %all-gather.2.cloned.1.call-done, s32[1024]{0:T(1024)S(1)} %get-tuple-element.34), kind=kCustom, calls=%fused_computation.6 | custom fusion | bytes 262160 | tf_op jit(solution)/shard_map/jit(_take)/gather | solution.py:91
  59.6 0.6 gather_fusion.6
  61.3 1.1 %fusion.3 = bf16[4,128,128]{2,0,1:T(4,128)(2,1)S(1)} fusion(f32[4,128,128]{2,0,1:T(4,128)S(1)} %convolution_add_fusion.1, f32[128,16,128]{2,0,1:T(8,128)S(1)} %convolution_bitcast_fusion, f32[4,128]{1,0:T(4,128)S(1)} %convert_bitcast_fusion, s32[16]{0:T(128)S(1)} %copy-done.17), kind=kOutput, calls=%fused_computation.17 | convolution fusion | flops 12779584 | bytes 1443904 | tf_op jit(solution)/shard_map/fti,tr->fri/dot_general | solution.py:30
  62.4 6.5 %all_gather.11 = bf16[256,512]{1,0:T(8,128)(2,1)S(1)} all-gather(bf16[128,512]{1,0:T(8,128)(2,1)S(1)} %bitcast.127), channel_id=1, replica_groups=mesh['dom'=16,'feat'=2] {'feat'}, dimensions={0}, use_global_device_ids=true | all-gather | bytes 393216 | tf_op jit(solution)/shard_map/all_gather | solution.py:106
  69.1 0.6 copy-done.5
  69.7 0.8 %fusion.4 = bf16[128,512]{1,0:T(8,128)(2,1)} fusion(f32[128,512]{1,0:T(8,128)S(1)} %convolution_bitcast_fusion.3, bf16[128,256]{1,0:T(8,128)(2,1)S(1)} %copy-done.5, bf16[256,512]{1,0:T(8,128)(2,1)S(1)} %all_gather.9, f32[128]{0:T(128)S(1)} %copy-done.12), kind=kOutput, calls=%fused_computation.18 | convolution fusion | flops 33816576 | bytes 721408 | tf_op jit(solution)/shard_map/dot_general | solution.py:99
  (100 shorter events, 6.3 us)
Async XLA Ops:
  6.5 15.0 %copy-start = (bf16[16,128,128]{2,1,0:T(8,128)(2,1)S(1)}, bf16[16,128,128]{2,1,0:T(8,128)(2,1)}, u32[]{:S(2)}) copy-start(bf16[16,128,128]{2,1,0:T(8,128)(2,1)} %param.30) | copy-start | bytes 1572868
  6.5 0.7 copy-start.14
  6.5 0.9 %copy-start.6 = (s32[1,16,16]{2,1,0:T(8,128)S(1)}, s32[1,16,16]{2,1,0:T(8,128)}, u32[]{:S(2)}) copy-start(s32[1,16,16]{2,1,0:T(8,128)} %param.24) | copy-start | bytes 3076
  6.5 51.2 %all-gather.2.cloned.1.call-start = ((), (), s32[]{:S(2)}) async-start(), calls=%async_computation | async-start | bytes 1114112 | tf_op jit(solution)/shard_map/all_gather | solution.py:90
  7.5 0.7 copy-start.7
  9.4 0.7 copy-start.13
  11.3 18.4 %collective-permute-start = (bf16[128,1,16]{0,2,1:T(8,128)(2,1)S(1)}, bf16[128,1,16]{0,2,1:T(8,128)(2,1)S(1)}, u32[]{:S(2)}, u32[]{:S(2)}) collective-permute-start(bf16[128,1,16]{0,2,1:T(8,128)(2,1)S(1)} %get-tuple-element.23), channel_id=1, source_target_pairs={{0,2},{2,0},{4,6},{6,4},{8,10},{10,8},{12,14},{14,12},{16,18},{18,... | collective-permute-start | bytes 12296 | tf_op jit(solution)/shard_map/ppermute | solution.py:71
  11.8 20.6 %collective-permute-start.1 = (bf16[128,1,16]{0,2,1:T(8,128)(2,1)S(1)}, bf16[128,1,16]{0,2,1:T(8,128)(2,1)S(1)}, u32[]{:S(2)}, u32[]{:S(2)}) collective-permute-start(bf16[128,1,16]{0,2,1:T(8,128)(2,1)S(1)} %get-tuple-element.22), channel_id=1, source_target_pairs={{0,4},{2,6},{4,0},{6,2},{8,12},{10,14},{12,8},{14,10},{16,20},{18,... | collective-permute-start | bytes 12296 | tf_op jit(solution)/shard_map/ppermute | solution.py:71
  14.4 18.1 %collective-permute-start.2 = (bf16[128,1,16]{0,2,1:T(8,128)(2,1)S(1)}, bf16[128,1,16]{0,2,1:T(8,128)(2,1)S(1)}, u32[]{:S(2)}, u32[]{:S(2)}) collective-permute-start(bf16[128,1,16]{0,2,1:T(8,128)(2,1)S(1)} %get-tuple-element.21), channel_id=1, source_target_pairs={{0,6},{2,4},{4,2},{6,0},{8,14},{10,12},{12,10},{14,8},{16,22},{18,... | collective-permute-start | bytes 12296 | tf_op jit(solution)/shard_map/ppermute | solution.py:71
  14.5 20.7 %collective-permute-start.3 = (bf16[128,1,16]{0,2,1:T(8,128)(2,1)S(1)}, bf16[128,1,16]{0,2,1:T(8,128)(2,1)S(1)}, u32[]{:S(2)}, u32[]{:S(2)}) collective-permute-start(bf16[128,1,16]{0,2,1:T(8,128)(2,1)S(1)} %get-tuple-element.20), channel_id=1, source_target_pairs={{0,8},{2,10},{4,12},{6,14},{8,0},{10,2},{12,4},{14,6},{16,24},{18,... | collective-permute-start | bytes 12296 | tf_op jit(solution)/shard_map/ppermute | solution.py:71
  16.3 19.0 %collective-permute-start.4 = (bf16[128,1,16]{0,2,1:T(8,128)(2,1)S(1)}, bf16[128,1,16]{0,2,1:T(8,128)(2,1)S(1)}, u32[]{:S(2)}, u32[]{:S(2)}) collective-permute-start(bf16[128,1,16]{0,2,1:T(8,128)(2,1)S(1)} %get-tuple-element.19), channel_id=1, source_target_pairs={{0,10},{2,8},{4,14},{6,12},{8,2},{10,0},{12,6},{14,4},{16,26},{18,... | collective-permute-start | bytes 12296 | tf_op jit(solution)/shard_map/ppermute | solution.py:71
  18.0 0.7 copy-start.15
  18.7 0.7 copy-start.9
  20.2 0.7 copy-start.8
  21.6 0.7 copy-start.10
  22.2 1.1 %copy-start.3 = (bf16[128,512]{1,0:T(8,128)(2,1)S(1)}, bf16[128,512]{1,0:T(8,128)(2,1)}, u32[]{:S(2)}) copy-start(bf16[128,512]{1,0:T(8,128)(2,1)} %param.22) | copy-start | bytes 393220
  29.7 9.1 %collective-permute-start.5 = (bf16[128,1,16]{0,2,1:T(8,128)(2,1)S(1)}, bf16[128,1,16]{0,2,1:T(8,128)(2,1)S(1)}, u32[]{:S(2)}, u32[]{:S(2)}) collective-permute-start(bf16[128,1,16]{0,2,1:T(8,128)(2,1)S(1)} %get-tuple-element.18), channel_id=1, source_target_pairs={{0,12},{2,14},{4,8},{6,10},{8,4},{10,6},{12,0},{14,2},{16,28},{18,... | collective-permute-start | bytes 12296 | tf_op jit(solution)/shard_map/ppermute | solution.py:71
  32.5 6.4 %collective-permute-start.6 = (bf16[128,1,16]{0,2,1:T(8,128)(2,1)S(1)}, bf16[128,1,16]{0,2,1:T(8,128)(2,1)S(1)}, u32[]{:S(2)}, u32[]{:S(2)}) collective-permute-start(bf16[128,1,16]{0,2,1:T(8,128)(2,1)S(1)} %get-tuple-element.17), channel_id=1, source_target_pairs={{0,14},{2,12},{4,10},{6,8},{8,6},{10,4},{12,2},{14,0},{16,30},{18,... | collective-permute-start | bytes 12296 | tf_op jit(solution)/shard_map/ppermute | solution.py:71
  32.5 9.3 %collective-permute-start.7 = (bf16[128,1,16]{0,2,1:T(8,128)(2,1)S(1)}, bf16[128,1,16]{0,2,1:T(8,128)(2,1)S(1)}, u32[]{:S(2)}, u32[]{:S(2)}) collective-permute-start(bf16[128,1,16]{0,2,1:T(8,128)(2,1)S(1)} %get-tuple-element.16), channel_id=1, source_target_pairs={{0,16},{2,18},{4,20},{6,22},{8,24},{10,26},{12,28},{14,30},{16,0},... | collective-permute-start | bytes 12296 | tf_op jit(solution)/shard_map/ppermute | solution.py:71
  35.2 7.4 %collective-permute-start.8 = (bf16[128,1,16]{0,2,1:T(8,128)(2,1)S(1)}, bf16[128,1,16]{0,2,1:T(8,128)(2,1)S(1)}, u32[]{:S(2)}, u32[]{:S(2)}) collective-permute-start(bf16[128,1,16]{0,2,1:T(8,128)(2,1)S(1)} %get-tuple-element.15), channel_id=1, source_target_pairs={{0,18},{2,16},{4,22},{6,20},{8,26},{10,24},{12,30},{14,28},{16,2},... | collective-permute-start | bytes 12296 | tf_op jit(solution)/shard_map/ppermute | solution.py:71
  35.3 11.7 %collective-permute-start.9 = (bf16[128,1,16]{0,2,1:T(8,128)(2,1)S(1)}, bf16[128,1,16]{0,2,1:T(8,128)(2,1)S(1)}, u32[]{:S(2)}, u32[]{:S(2)}) collective-permute-start(bf16[128,1,16]{0,2,1:T(8,128)(2,1)S(1)} %get-tuple-element.14), channel_id=1, source_target_pairs={{0,20},{2,22},{4,16},{6,18},{8,28},{10,30},{12,24},{14,26},{16,4},... | collective-permute-start | bytes 12296 | tf_op jit(solution)/shard_map/ppermute | solution.py:71
  38.8 8.2 %collective-permute-start.10 = (bf16[128,1,16]{0,2,1:T(8,128)(2,1)S(1)}, bf16[128,1,16]{0,2,1:T(8,128)(2,1)S(1)}, u32[]{:S(2)}, u32[]{:S(2)}) collective-permute-start(bf16[128,1,16]{0,2,1:T(8,128)(2,1)S(1)} %get-tuple-element.13), channel_id=1, source_target_pairs={{0,22},{2,20},{4,18},{6,16},{8,30},{10,28},{12,26},{14,24},{16,6},... | collective-permute-start | bytes 12296 | tf_op jit(solution)/shard_map/ppermute | solution.py:71
  38.9 8.2 %collective-permute-start.11 = (bf16[128,1,16]{0,2,1:T(8,128)(2,1)S(1)}, bf16[128,1,16]{0,2,1:T(8,128)(2,1)S(1)}, u32[]{:S(2)}, u32[]{:S(2)}) collective-permute-start(bf16[128,1,16]{0,2,1:T(8,128)(2,1)S(1)} %get-tuple-element.12), channel_id=1, source_target_pairs={{0,24},{2,26},{4,28},{6,30},{8,16},{10,18},{12,20},{14,22},{16,8},... | collective-permute-start | bytes 12296 | tf_op jit(solution)/shard_map/ppermute | solution.py:71
  41.8 5.2 %collective-permute-start.12 = (bf16[128,1,16]{0,2,1:T(8,128)(2,1)S(1)}, bf16[128,1,16]{0,2,1:T(8,128)(2,1)S(1)}, u32[]{:S(2)}, u32[]{:S(2)}) collective-permute-start(bf16[128,1,16]{0,2,1:T(8,128)(2,1)S(1)} %get-tuple-element.11), channel_id=1, source_target_pairs={{0,26},{2,24},{4,30},{6,28},{8,18},{10,16},{12,22},{14,20},{16,10}... | collective-permute-start | bytes 12296 | tf_op jit(solution)/shard_map/ppermute | solution.py:71
  42.5 6.3 %collective-permute-start.13 = (bf16[128,1,16]{0,2,1:T(8,128)(2,1)S(1)}, bf16[128,1,16]{0,2,1:T(8,128)(2,1)S(1)}, u32[]{:S(2)}, u32[]{:S(2)}) collective-permute-start(bf16[128,1,16]{0,2,1:T(8,128)(2,1)S(1)} %get-tuple-element.10), channel_id=1, source_target_pairs={{0,28},{2,30},{4,24},{6,26},{8,20},{10,22},{12,16},{14,18},{16,12}... | collective-permute-start | bytes 12296 | tf_op jit(solution)/shard_map/ppermute | solution.py:71
  47.0 5.7 %collective-permute-start.14 = (bf16[128,1,16]{0,2,1:T(8,128)(2,1)S(1)}, bf16[128,1,16]{0,2,1:T(8,128)(2,1)S(1)}, u32[]{:S(2)}, u32[]{:S(2)}) collective-permute-start(bf16[128,1,16]{0,2,1:T(8,128)(2,1)S(1)} %get-tuple-element.9), channel_id=1, source_target_pairs={{0,30},{2,28},{4,26},{6,24},{8,22},{10,20},{12,18},{14,16},{16,14}... | collective-permute-start | bytes 12296 | tf_op jit(solution)/shard_map/ppermute | solution.py:71
  53.4 1.1 %copy-start.1 = (bf16[16,128,128]{2,1,0:T(8,128)(2,1)S(1)}, bf16[16,128,128]{2,1,0:T(8,128)(2,1)}, u32[]{:S(2)}) copy-start(bf16[16,128,128]{2,1,0:T(8,128)(2,1)} %param.33) | copy-start | bytes 1572868
  59.6 1.0 %copy-start.2 = (bf16[16,128,128]{2,1,0:T(8,128)(2,1)S(1)}, bf16[16,128,128]{2,1,0:T(8,128)(2,1)}, u32[]{:S(2)}) copy-start(bf16[16,128,128]{2,1,0:T(8,128)(2,1)} %param.36) | copy-start | bytes 1572868
  60.6 0.7 copy-start.17
  62.4 6.5 %copy-start.4 = (bf16[128,256]{1,0:T(8,128)(2,1)S(1)}, bf16[128,256]{1,0:T(8,128)(2,1)}, u32[]{:S(2)}) copy-start(bf16[128,256]{1,0:T(8,128)(2,1)} %param.38) | copy-start | bytes 196612
  68.9 0.8 %copy-start.5 = (bf16[128,256]{1,0:T(8,128)(2,1)S(1)}, bf16[128,256]{1,0:T(8,128)(2,1)}, u32[]{:S(2)}) copy-start(bf16[128,256]{1,0:T(8,128)(2,1)} %param.37) | copy-start | bytes 196612
  68.9 0.8 %copy-start.12 = (f32[128]{0:T(128)S(1)}, f32[128]{0:T(128)}, u32[]{:S(2)}) copy-start(f32[128]{0:T(128)} %param.39) | copy-start | bytes 1540
  (2 other events, 1.3 us)
Sparse Core Ops, SparseCore 0:
  18.2 39.4 all-gather.1
